TPU v7x, 128 devices: a whole 4x4x4 slice. The times are simulated.
128 devices in a mesh: width: 16 (over x_lo, z, core), token: 4 (over y), query: 2 (over x_hi).
Axes of the slice: x: 4 (x_hi: 2, x_lo: 2; x = x_hi * 2 + x_lo), y: 4, z: 4, core: 2. Of those that a mesh axis runs over, the one named last changes fastest.
Arguments:
- layer_inputs: bfloat16 [1536, 8192], P(('token', 'query'), 'width'), may hold values from -20 to 20
- out_grads: bfloat16 [1536, 8192], P(('token', 'query'), 'width'), may hold values from -20 to 20
- basis_in: bfloat16 [8192, 8192], P(None, 'width'), may hold values from -0.125 to 0.125
- basis_out: bfloat16 [8192, 8192], P(None, 'width'), may hold values from -0.125 to 0.125
- query_in: bfloat16 [256, 32, 8192], P('query', None, 'width'), may hold values from -0.03125 to 0.03125
- query_out: bfloat16 [256, 32, 8192], P('query', None, 'width'), may hold values from -0.03125 to 0.03125
Outputs:
- scores: float32 [256, 1536], P('query', 'token')
All inputs are finite; a program needn't handle non-finite values.
Results may differ from a plain program's by a relative error of at most 0.0003.
Values may be sent and summed in bfloat16 or wider, within the bound.
A program may use at most 128 MiB of HBM per device.

v0:
```python
import jax
import jax.numpy as jnp
from jax import lax
from jax.sharding import PartitionSpec as P

damping = 0.1


def side_by_side(arrays, axis, dim, along):
    ends, at = ([], 0)
    for a in arrays[:-1]:
        at += a.shape[along]
        ends.append(at)
    both = jnp.concatenate(arrays, axis=along)
    return tuple(jnp.split(lax.all_gather(both, axis, axis=dim, tiled=True), ends, axis=along))


def from_everyone(x, axis):
    size = lax.axis_size(axis)
    return lax.all_to_all(jnp.broadcast_to(x[None], (size, *x.shape)), axis, 0, 0, tiled=True)


def over_copies(x, axis):
    return from_everyone(x, axis).sum(axis=0)


def together(arrays, axis):
    line, at, outs = (jnp.concatenate([a.reshape(-1) for a in arrays]), 0, [])
    so_far = over_copies(line, axis)
    for a in arrays:
        outs.append(so_far[at : at + a.size].reshape(a.shape))
        at += a.size
    return tuple(outs)


def laid_out(tiles, dim):
    tiles = jnp.moveaxis(tiles, 0, dim)
    shape = tiles.shape
    return tiles.reshape(*shape[:dim], shape[dim] * shape[dim + 1], *shape[dim + 2 :])


def gathered_copies(x, axis, dim):
    return laid_out(from_everyone(x, axis), dim)


def side_by_side_2(arrays, axis, dim, along):
    widths = [a.shape[along] for a in arrays]
    both = jnp.concatenate(arrays, axis=along)
    whole = gathered_copies(both, axis, dim)
    return tuple(jnp.split(whole, [sum(widths[:k]) for k in range(1, len(widths))], axis=along))


def on_device(layer_inputs, out_grads, basis_in, basis_out, query_in, query_out):
    width_cols = basis_in.shape[1]
    full_in, full_out = side_by_side((layer_inputs, out_grads), "width", 1, 0)
    rotated_in = jnp.dot(full_in, basis_in, preferred_element_type=jnp.float32)
    rotated_out = jnp.dot(full_out, basis_out, preferred_element_type=jnp.float32)
    total_tokens = layer_inputs.shape[0] * lax.axis_size("token") * lax.axis_size("query")
    squares_in, squares_out = together(
        (jnp.sum(rotated_in * rotated_in, axis=0), jnp.sum(rotated_out * rotated_out, axis=0)),
        ("token", "query"),
    )
    scaled_in = rotated_in / (squares_in / total_tokens + damping)
    scaled_out = rotated_out / (squares_out / total_tokens + damping)
    group_in, group_out = side_by_side_2((scaled_in, scaled_out), "query", 0, 1)
    group_tokens = group_in.shape[0]
    rank_count = query_in.shape[1]
    flat_in = query_in.reshape(-1, width_cols)
    flat_out = query_out.reshape(-1, width_cols)
    rows_in = flat_in.astype(jnp.float32)
    rows_out = flat_out.astype(jnp.float32)
    product_in = lax.dot_general(
        rows_in,
        group_in,
        (((1,), (1,)), ((), ())),
        precision=lax.Precision.HIGHEST,
        preferred_element_type=jnp.float32,
    )
    product_out = lax.dot_general(
        rows_out,
        group_out,
        (((1,), (1,)), ((), ())),
        precision=lax.Precision.HIGHEST,
        preferred_element_type=jnp.float32,
    )
    shares = lax.psum_scatter(
        jnp.concatenate([product_in, product_out], axis=1), "width", scatter_dimension=0, tiled=True
    )
    joined = shares[:, :group_tokens] * shares[:, group_tokens:]
    score_block = joined.reshape(-1, rank_count, group_tokens).sum(axis=1)
    return gathered_copies(score_block, "width", 0)


def solution(mesh):
    return jax.shard_map(
        on_device,
        mesh=mesh,
        in_specs=(
            P(("token", "query"), "width"),
            P(("token", "query"), "width"),
            P(None, "width"),
            P(None, "width"),
            P("query", None, "width"),
            P("query", None, "width"),
        ),
        out_specs=P("query", "token"),
        check_vma=False,
    )
```

profile of v0, /device:TPU:1, one launch (start us, length us, event | category | flops | bytes accessed | tf_op | source)
XLA Modules:
  0.0 227.3 jit_solution(4946059594369474203)
XLA Ops:
  6.5 0.0 all-gather.2.cloned.1.call-start
  6.5 1.8 pad_maximum_fusion.2
  8.4 0.0 all-gather.2.cloned.1.call-update
  8.4 0.0 reduce-scatter.2.cloned.1.call-start
  8.4 46.7 %all-gather.2.cloned.1.call-done = bf16[384,8192]{1,0:T(8,128)(2,1)} async-done(((bf16[384,512]{1,0:T(8,128)(2,1)}), bf16[384,8192]{1,0:T(8,128)(2,1)}) %all-gather.2.cloned.1.call-update) | async-done | bytes 6291472 | tf_op jit(solution)/shard_map/all_gather | solution.py:15
  55.1 0.0 copy-start.2
  55.1 6.3 %multiply_reduce_fusion = (f32[512]{0:T(512)S(1)}, f32[192,512]{1,0:T(8,128)S(1)}) fusion(bf16[8192,512]{1,0:T(8,128)(2,1)} %param.9, bf16[384,8192]{1,0:T(8,128)(2,1)} %all-gather.2.cloned.1.call-done), kind=kOutput, calls=%fused_computation.13 | convolution fusion | flops 1610808832 | bytes 11929600 | tf_op jit(solution)/shard_map/dot_general | solution.py:57
  61.4 0.0 copy-done.2
  61.4 5.2 %multiply_reduce_fusion.1 = (f32[512]{0:T(512)S(1)}, f32[192,512]{1,0:T(8,128)S(1)}) fusion(bf16[8192,512]{1,0:T(8,128)(2,1)} %param.8, bf16[384,8192]{1,0:T(8,128)(2,1)S(1)} %copy-done.2), kind=kOutput, calls=%fused_computation.14 | convolution fusion | flops 1610808832 | bytes 11929600 | tf_op jit(solution)/shard_map/dot_general | solution.py:56
  66.6 12.6 %all_to_all.16 = f32[8,1,1024]{2,1,0:T(1,128)S(1)} all-to-all(f32[8,1,1024]{2,1,0:T(1,128)S(1)} %broadcast_in_dim.6), channel_id=1, replica_groups=mesh['width'=16,'token'=4,'query'=2] {'token','query'}, dimensions={0} | all-to-all | bytes 65536 | tf_op jit(solution)/shard_map/all_to_all | solution.py:20
  79.3 0.0 copy-start
  79.3 0.1 broadcast_divide_fusion
  79.4 0.1 pad_maximum_fusion.1
  79.5 0.2 broadcast_in_dim.7
  79.7 21.9 %all_to_all.17 = f32[2,192,1024]{2,1,0:T(8,128)S(1)} all-to-all(f32[2,192,1024]{2,1,0:T(8,128)S(1)} %broadcast_in_dim.7), channel_id=1, replica_groups=mesh['width'=16,'token'=4,'query'=2] {'query'}, dimensions={0} | all-to-all | bytes 3145728 | tf_op jit(solution)/shard_map/all_to_all | solution.py:20
  101.5 0.0 copy-start.1
  101.5 0.0 copy-done
  101.5 7.2 %convolution_bitcast_fusion = f32[4096,384]{0,1:T(8,128)} fusion(bf16[4096,512]{1,0:T(8,128)(2,1)S(1)} %bitcast.16, f32[384,1024]{1,0:T(8,128)S(1)} %bitcast.14), kind=kOutput, calls=%fused_computation.1 | convolution fusion | flops 9663676416 | bytes 11272192 | tf_op jit(solution)/shard_map/dot_general | solution.py:79
  108.7 0.0 copy-done.1
  108.7 7.3 %convolution_bitcast_fusion.1 = f32[4096,384]{0,1:T(8,128)} fusion(bf16[4096,512]{1,0:T(8,128)(2,1)S(1)} %bitcast.17, f32[384,1024]{1,0:T(8,128)S(1)} %bitcast.15), kind=kOutput, calls=%fused_computation.2 | convolution fusion | flops 9663676416 | bytes 11272192 | tf_op jit(solution)/shard_map/dot_general | solution.py:72
  116.0 10.7 %pad_maximum_fusion = f32[4096,768]{0,1:T(8,128)} fusion(f32[4096,384]{0,1:T(8,128)} %convolution_bitcast_fusion, f32[4096,384]{0,1:T(8,128)} %convolution_bitcast_fusion.1), kind=kLoop, calls=%fused_computation | loop fusion | flops 3145728 | bytes 25165824 | tf_op jit(solution)/shard_map/concatenate | solution.py:87
  126.8 0.0 reduce-scatter.2.cloned.1.call-update
  126.8 78.5 %reduce-scatter.2.cloned.1.call-done = f32[256,768]{0,1:T(8,128)} async-done(((f32[4096,768]{0,1:T(8,128)}), f32[256,768]{0,1:T(8,128)}) %reduce-scatter.2.cloned.1.call-update) | async-done | bytes 786448 | tf_op jit(solution)/shard_map/reduce_scatter | solution.py:86
  205.3 1.2 slice_multiply_fusion
  206.5 0.2 copy.10
  206.7 13.1 %all_to_all.18 = f32[16,8,384]{2,1,0:T(8,128)S(1)} all-to-all(f32[16,8,384]{2,1,0:T(8,128)S(1)} %broadcast_in_dim.8), channel_id=1, replica_groups=mesh['width'=16,'token'=4,'query'=2] {'width'}, dimensions={0} | all-to-all | bytes 393216 | tf_op jit(solution)/shard_map/all_to_all | solution.py:20
  219.8 0.7 copy.15
  (6 shorter events, 0.1 us)
Async XLA Ops:
  6.5 48.6 %all-gather.2.cloned.1.call-start = ((), (), s32[]{:S(2)}) async-start(), calls=%async_computation.4 | async-start | bytes 6684672 | tf_op jit(solution)/shard_map/all_gather | solution.py:15
  8.4 196.9 %reduce-scatter.2.cloned.1.call-start = ((), (), s32[]{:S(2)}) async-start(), calls=%async_computation.5 | async-start | bytes 13369344 | tf_op jit(solution)/shard_map/reduce_scatter | solution.py:86
  55.1 6.3 %copy-start.2 = (bf16[384,8192]{1,0:T(8,128)(2,1)S(1)}, bf16[384,8192]{1,0:T(8,128)(2,1)}, u32[]{:S(2)}) copy-start(bf16[384,8192]{1,0:T(8,128)(2,1)} %all-gather.2.cloned.1.call-done) | copy-start | bytes 18874372
  79.3 22.3 %copy-start = (bf16[128,32,512]{2,1,0:T(8,128)(2,1)S(1)}, bf16[128,32,512]{2,1,0:T(8,128)(2,1)}, u32[]{:S(2)}) copy-start(bf16[128,32,512]{2,1,0:T(8,128)(2,1)} %param.11) | copy-start | bytes 12582916
  101.5 7.2 %copy-start.1 = (bf16[128,32,512]{2,1,0:T(8,128)(2,1)S(1)}, bf16[128,32,512]{2,1,0:T(8,128)(2,1)}, u32[]{:S(2)}) copy-start(bf16[128,32,512]{2,1,0:T(8,128)(2,1)} %param.10) | copy-start | bytes 12582916
Sparse Core Ops, SparseCore 0:
  9.0 46.0 all-gather.1
  126.9 78.3 reduce-scatter.1
where the time goes:
time: 228 us; the launch traced here: 227 us
  waiting for transfers between devices  125 us (55%)
  blocking collectives  47.6 us (21%)
  matrix products  25.9 us (11%)
  other arithmetic  14 us (6%)
  between operations  13.5 us (6%)
    reduce_scatter x1, waiting for transfers between devices, on_device(): lax.psum_scatter(jnp.concatenate([product_in, product_out], axis=1), 'wid...  78.5 us
    all_to_all x3, blocking collectives, from_everyone(): lax.all_to_all(jnp.broadcast_to(x[None], (size, *x.shape)), axis, 0, 0, t...  47.6 us
    all_gather x1, waiting for transfers between devices, side_by_side(): lax.all_gather(both, axis, axis=dim, tiled=True)  46.7 us
    concatenate x1, other arithmetic, on_device(): jnp.concatenate([product_in, product_out], axis=1)  10.7 us
    dot_general x1, matrix products, on_device(): lax.dot_general(rows_in, group_in, (((1,), (1,)), ((), ())), precision=la...  7.27 us
    dot_general x1, matrix products, on_device(): lax.dot_general(rows_out, group_out, (((1,), (1,)), ((), ())), precision=...  7.2 us
    dot_general x1, matrix products, on_device(): jnp.dot(full_out, basis_out, preferred_element_type=jnp.float32)  6.28 us
    dot_general x1, matrix products, on_device(): rotated_in = jnp.dot(full_in, basis_in, preferred_element_type=jnp.float32)  5.19 us
  transfers between devices with their start and end apart: 2, of which 2 were waited for; matrix products, arithmetic and copies ran while one was open for 0% of the time, Pallas kernels for 0%

commit v1 on v0

v1 whole, which is shorter than its diff:
```python
import jax
import jax.numpy as jnp
from jax import lax
from jax.experimental import pallas as pl
from jax.experimental.pallas import tpu as pltpu
from jax.sharding import PartitionSpec as P

damping = 0.1
MESH = pl.DeviceIdType.MESH
N_SEM = 160
NT = (((1,), (1,)), ((), ()))


def kernel(total_tokens, li, og, bi, bo, qi, qo, out, X, BAS, A, ACC, AR, S, PS, RF, RN, PR, SC, ss, rs, lx, lb, la):
    acts, bases, queries = (li, og), (bi, bo), (qi, qo)
    w, t, q = lax.axis_index("width"), lax.axis_index("token"), lax.axis_index("query")
    x, z, c = w // 8, lax.rem(w // 2, 4), lax.rem(w, 2)
    xq, cq = 1 - x, 1 - c
    zu, zd, zf = lax.rem(z + 1, 4), lax.rem(z + 3, 4), lax.rem(z + 2, 4)
    tu, td, tf = lax.rem(t + 1, 4), lax.rem(t + 3, 4), lax.rem(t + 2, 4)

    def at(px, pz, pc):
        return (px * 4 + pz) * 2 + pc

    dev_x, dev_c = {"width": at(xq, z, c)}, {"width": at(x, z, cq)}
    dev_u, dev_d = {"width": at(x, zu, c)}, {"width": at(x, zd, c)}
    dev_o = {"width": at(xq, z, c), "query": 1 - q}
    dev_tu, dev_td = {"token": tu}, {"token": td}
    half = X.shape[2] // 2
    rows = X.shape[2]
    upper, lower = pl.ds(0, half), pl.ds(half, half)

    keys, pending = {}, []

    def number(key):
        return keys.setdefault(key, len(keys))

    def send(key, src, dst, dev):
        i = number(key)
        copy = pltpu.make_async_remote_copy(
            src_ref=src, dst_ref=dst, send_sem=ss.at[i], recv_sem=rs.at[i], device_id=dev, device_id_type=MESH
        )
        copy.start()
        pending.append(copy)

    def arrive(key, region, dev=None):
        i = number(key)
        pltpu.make_async_remote_copy(
            src_ref=region, dst_ref=region, send_sem=ss.at[i], recv_sem=rs.at[i],
            device_id=dev_c if dev is None else dev, device_id_type=MESH,
        ).wait_recv()

    me = at(x, z, c)
    own_x = [pltpu.make_async_copy(acts[a], X.at[a, me], lx.at[a]) for a in range(2)]
    for cp in own_x:
        cp.start()
    order = [(x, z), (xq, z), (x, zd), (x, zu), (xq, zd), (xq, zu), (x, zf), (xq, zf)]
    base_copies = {}
    for a in range(2):
        for n, (px, pz) in enumerate(order):
            pair = pl.ds((px * 4 + pz) * 2, 2)
            base_copies[a, n] = pltpu.make_async_copy(bases[a].at[pair], BAS.at[a, pair], lb.at[a, n])
            base_copies[a, n].start()
    src_me = x * 2 + c
    own_a = [pltpu.make_async_copy(queries[a].at[x, :, c], A.at[a, src_me], la.at[a]) for a in range(2)]
    for cp in own_a:
        cp.start()

    barrier = pltpu.get_barrier_semaphore()
    met = 0
    for d in range(1, 16):
        pl.semaphore_signal(barrier, inc=1, device_id={"width": lax.rem(w + d, 16)}, device_id_type=MESH)
        met += 1
    eight = t * 2 + q
    mates = []
    for d in range(1, 8):
        m = lax.rem(eight + d, 8)
        mates.append((m, {"token": m // 2, "query": lax.rem(m, 2)}))
        pl.semaphore_signal(barrier, inc=1, device_id=mates[-1][1], device_id_type=MESH)
        met += 1
    pl.semaphore_signal(barrier, inc=1, device_id=dev_o, device_id_type=MESH)
    met += 1
    pl.semaphore_wait(barrier, met)

    done_pairs = [0, 0]

    def rotate(a, n):
        base_copies[a, n].wait()
        px, pz = order[n]
        first = (px * 4 + pz) * 2
        for col in range(0, 512, 256):
            cols = pl.ds(col, 256)
            part = jnp.dot(X[a, first], BAS[a, first, :, cols], preferred_element_type=jnp.float32)
            part += jnp.dot(X[a, first + 1], BAS[a, first + 1, :, cols], preferred_element_type=jnp.float32)
            if done_pairs[a]:
                part += ACC[a, :, cols]
            ACC[a, :, cols] = part
        done_pairs[a] += 1

    def open_x(a):
        own_x[a].wait()
        send(("x", a), X.at[a, me], X.at[a, me], dev_x)
        send(("c", a), X.at[a, me], X.at[a, me], dev_c)

    def open_z(a):
        send(("zu", a), X.at[a, me], X.at[a, me], dev_u)
        send(("zd", a), X.at[a, me], X.at[a, me], dev_d)

    def from_core(key, a, px, pz):
        arrive(key, X.at[a, at(px, pz, cq)])

    def to_core(key, a, px, pz):
        blk = X.at[a, at(px, pz, c)]
        send(key, blk, blk, dev_c)

    def step1(a):
        blk = X.at[a, at(xq, z, c)]
        arrive(("x", a), blk)
        send(("xzu", a), blk, blk, dev_u)
        send(("xzd", a), blk, blk, dev_d)
        to_core(("cx", a), a, xq, z)
        from_core(("c", a), a, x, z)
        rotate(a, 0)
        from_core(("cx", a), a, xq, z)
        rotate(a, 1)

    def step2(a, px, tag, n):
        up, down = at(px, zd, c), at(px, zu, c)
        arrive((tag + "zu", a), X.at[a, up])
        send((tag + "fu", a), X.at[a, up, upper], X.at[a, up, upper], dev_u)
        to_core((tag + "czu", a), a, px, zd)
        arrive((tag + "zd", a), X.at[a, down])
        send((tag + "fd", a), X.at[a, down, lower], X.at[a, down, lower], dev_d)
        to_core((tag + "czd", a), a, px, zu)
        from_core((tag + "czu", a), a, px, zd)
        rotate(a, n)
        from_core((tag + "czd", a), a, px, zu)
        rotate(a, n + 1)

    def step3(a, px, tag, n):
        far = at(px, zf, c)
        arrive((tag + "fu", a), X.at[a, far, upper])
        arrive((tag + "fd", a), X.at[a, far, lower])
        to_core((tag + "cf", a), a, px, zf)
        from_core((tag + "cf", a), a, px, zf)
        rotate(a, n)

    def squares(a):
        val = ACC[a]
        AR[a, eight] = jnp.sum((val * val).reshape(rows // 8, 8, 512), axis=0)
        for d, (m, dev) in enumerate(mates):
            send(("ar", a, d), AR.at[a, eight], AR.at[a, eight], dev)

    def scale(a):
        for d in range(7):
            arrive(("ar", a, d), AR.at[a, lax.rem(eight + 7 - d, 8)])
        tot = AR[a, 0]
        for k in range(1, 8):
            tot += AR[a, k]
        inv = 1.0 / (jnp.sum(tot, axis=0, keepdims=True) / total_tokens + damping)
        val = ACC[a] * inv
        hi = val.astype(jnp.bfloat16)
        S[a, q, src_me, pl.ds(0, rows)] = hi
        S[a, q, src_me, pl.ds(rows, rows)] = (val - hi.astype(jnp.float32)).astype(jnp.bfloat16)
        blk = S.at[a, q, src_me]
        send(("bx", a), blk, blk, dev_x)
        send(("bo", a), blk, blk, dev_o)
        send(("bc", a), blk, blk, dev_c)

    his, los = pl.ds(0, rows), pl.ds(rows, rows)
    p = 1 - q

    def share(a):
        bx = S.at[a, q, xq * 2 + c]
        arrive(("bx", a), bx)
        hi = S.at[a, q, xq * 2 + c, his]
        send(("bh", a), hi, hi, dev_o)
        send(("bcx", a), bx, bx, dev_c)
        bo_ = S.at[a, p, xq * 2 + c]
        arrive(("bo", a), bo_)
        lo = S.at[a, p, xq * 2 + c, los]
        send(("bl", a), lo, lo, dev_x)
        send(("bco", a), bo_, bo_, dev_c)

    def share_far(a):
        arrive(("bh", a), S.at[a, p, x * 2 + c, his])
        arrive(("bl", a), S.at[a, p, x * 2 + c, los])
        blk = S.at[a, p, x * 2 + c]
        send(("bcf", a), blk, blk, dev_c)

    def own_ready(a):
        arrive(("bc", a), S.at[a, q, x * 2 + cq])
        arrive(("bcx", a), S.at[a, q, xq * 2 + cq])

    def other_ready(a):
        arrive(("bco", a), S.at[a, p, xq * 2 + cq])
        arrive(("bcf", a), S.at[a, p, x * 2 + cq])

    def open_a(a):
        send(("ac", a), queries[a].at[x, :, cq], A.at[a, src_me], dev_c)

    def open_ax(a):
        for k in range(2):
            send_ax(a, k)

    def send_ax(a, k):
        pc = c if k == 0 else cq
        send(("ax", a, k), queries[a].at[xq, t, pc], A.at[a, src_me, t], {"width": at(xq, z, pc)})

    def spread_a(a):
        for k in range(2):
            pc = c if k == 0 else cq
            arrive(("ax", a, k), A.at[a, xq * 2 + pc, t])
        both = pl.ds(xq * 2, 2)
        send(("ayu", a), A.at[a, both, t], A.at[a, both, t], dev_tu)
        send(("ayd", a), A.at[a, both, t], A.at[a, both, t], dev_td)

    def spread_a2(a):
        both = pl.ds(xq * 2, 2)
        arrive(("ayu", a), A.at[a, both, td])
        one = A.at[a, xq * 2, td]
        send(("agu", a), one, one, dev_tu)
        arrive(("ayd", a), A.at[a, both, tu])
        two = A.at[a, xq * 2 + 1, tu]
        send(("agd", a), two, two, dev_td)

    def a_ready(a):
        own_a[a].wait()
        arrive(("ac", a), A.at[a, x * 2 + cq])
        arrive(("agu", a), A.at[a, xq * 2, tf])
        arrive(("agd", a), A.at[a, xq * 2 + 1, tf])

    def pair(a, h, zz):
        hq = q if h == 0 else p
        acc = None
        for k in range(4):
            part = lax.dot_general(S[a, hq, k], A[a, k, zz], NT, preferred_element_type=jnp.float32)
            acc = part if acc is None else acc + part
        PS[a, h, zz] = acc[:rows] + acc[rows:]

    def pairs(a, h):
        pair(a, h, zf)
        send(("pfu", a, h), PS.at[a, h, zf, upper], RF.at[a, h, 0], dev_u)
        send(("pfd", a, h), PS.at[a, h, zf, lower], RF.at[a, h, 1], dev_d)
        pair(a, h, zu)
        pair(a, h, zd)
        arrive(("pfu", a, h), RF.at[a, h, 0])
        PS[a, h, zu, upper] += RF[a, h, 0]
        send(("pnu", a, h), PS.at[a, h, zu], RN.at[a, h, 0], dev_u)
        arrive(("pfd", a, h), RF.at[a, h, 1])
        PS[a, h, zd, lower] += RF[a, h, 1]
        send(("pnd", a, h), PS.at[a, h, zd], RN.at[a, h, 1], dev_d)
        pair(a, h, z)

    def whole(a, h):
        arrive(("pnu", a, h), RN.at[a, h, 0])
        arrive(("pnd", a, h), RN.at[a, h, 1])
        return PS[a, h, z] + RN[a, h, 0] + RN[a, h, 1]

    open_x(0)
    open_z(0)
    open_x(1)
    open_ax(0)
    open_a(0)
    open_a(1)
    step1(0)
    step2(0, x, "", 2)
    step2(0, xq, "x", 4)
    open_z(1)
    step3(0, x, "", 6)
    step3(0, xq, "x", 7)
    squares(0)
    step1(1)
    step2(1, x, "", 2)
    scale(0)
    open_ax(1)
    spread_a(0)
    step2(1, xq, "x", 4)
    step3(1, x, "", 6)
    step3(1, xq, "x", 7)
    squares(1)
    share(0)
    spread_a2(0)
    own_ready(0)
    scale(1)
    share_far(0)
    a_ready(0)
    pairs(0, 0)
    other_ready(0)
    spread_a(1)
    pairs(0, 1)
    share(1)
    spread_a2(1)
    own_ready(1)
    share_far(1)
    a_ready(1)
    pairs(1, 0)
    other_ready(1)
    pairs(1, 1)
    for h in range(2):
        hq = q if h == 0 else p
        PR[pl.ds(hq * rows, rows)] = whole(0, h) * whole(1, h)
    ranks = 32
    pick = (
        lax.broadcasted_iota(jnp.int32, (8, 256), 1) // ranks == lax.broadcasted_iota(jnp.int32, (8, 256), 0)
    ).astype(jnp.float32)
    SC[w] = lax.dot_general(
        pick, PR[...], NT, precision=lax.Precision.HIGHEST, preferred_element_type=jnp.float32
    )
    for d in range(1, 16):
        send(("sc", d), SC.at[w], SC.at[w], {"width": lax.rem(w + d, 16)})
    for d in range(1, 16):
        arrive(("sc", d), SC.at[lax.rem(w + 16 - d, 16)])
    out[...] = SC[...]
    for copy in pending:
        copy.wait_send()
    assert len(keys) <= N_SEM


def on_device(layer_inputs, out_grads, basis_in, basis_out, query_in, query_out):
    total_tokens = layer_inputs.shape[0] * lax.axis_size("token") * lax.axis_size("query")
    rows, cols = layer_inputs.shape
    f32, bf16 = jnp.float32, jnp.bfloat16
    hbm = pl.BlockSpec(memory_space=pl.ANY)
    scores = pl.pallas_call(
        lambda *refs: kernel(total_tokens, *refs),
        out_shape=jax.ShapeDtypeStruct((16, 8, 2 * rows), f32),
        in_specs=[hbm] * 6,
        out_specs=pl.BlockSpec(memory_space=pltpu.VMEM),
        scratch_shapes=[
            pltpu.VMEM((2, 16, rows, cols), bf16),
            pltpu.VMEM((2, 16, cols, cols), bf16),
            pltpu.VMEM((2, 4, 4, 256, cols), bf16),
            pltpu.VMEM((2, rows, cols), f32),
            pltpu.VMEM((2, 8, 8, cols), f32),
            pltpu.VMEM((2, 2, 4, 2 * rows, cols), bf16),
            pltpu.VMEM((2, 2, 4, rows, 256), f32),
            pltpu.VMEM((2, 2, 2, rows // 2, 256), f32),
            pltpu.VMEM((2, 2, 2, rows, 256), f32),
            pltpu.VMEM((2 * rows, 256), f32),
            pltpu.VMEM((16, 8, 2 * rows), f32),
            pltpu.SemaphoreType.DMA((N_SEM,)),
            pltpu.SemaphoreType.DMA((N_SEM,)),
            pltpu.SemaphoreType.DMA((2,)),
            pltpu.SemaphoreType.DMA((2, 8)),
            pltpu.SemaphoreType.DMA((2,)),
        ],
        compiler_params=pltpu.CompilerParams(
            collective_id=0, has_side_effects=True, vmem_limit_bytes=60 * 1024 * 1024
        ),
        name="influence",
    )(
        layer_inputs,
        out_grads,
        basis_in.reshape(16, cols, cols),
        basis_out.reshape(16, cols, cols),
        query_in.reshape(2, 4, 2, 256, cols),
        query_out.reshape(2, 4, 2, 256, cols),
    )
    return scores.reshape(128, 2 * rows)


def solution(mesh):
    return jax.shard_map(
        on_device,
        mesh=mesh,
        in_specs=(
            P(("token", "query"), "width"),
            P(("token", "query"), "width"),
            P(None, "width"),
            P(None, "width"),
            P("query", None, "width"),
            P("query", None, "width"),
        ),
        out_specs=P("query", "token"),
        check_vma=False,
    )
```

time: 228 us -> 117 us (0.51)
  waiting for transfers between devices: 125 us -> 0 us
  Pallas kernels: 0 us -> 115 us
  blocking collectives: 47.6 us -> 0 us
  matrix products: 25.9 us -> 0 us
  other arithmetic: 14 us -> 0 us
  between operations: 13.5 us -> 0.01 us
    pallas_call x0 -> x1, Pallas kernels: none -> 115 us  [on_device(): pl.pallas_call(lambda *refs: kernel(total_tokens, *refs), out_shape=jax.S...]
    reduce_scatter x1 -> x0, waiting for transfers between devices: 78.5 us -> none  [on_device(): lax.psum_scatter(jnp.concatenate([product_in, product_out], axis=1), 'wid...]
    all_to_all x3 -> x0, blocking collectives: 47.6 us -> none  [from_everyone(): lax.all_to_all(jnp.broadcast_to(x[None], (size, *x.shape)), axis, 0, 0, t...]
    all_gather x1 -> x0, waiting for transfers between devices: 46.7 us -> none  [side_by_side(): lax.all_gather(both, axis, axis=dim, tiled=True)]
    dot_general x4 -> x0, matrix products: 25.9 us -> none  [the longest x1 7.27 us: on_device(): lax.dot_general(rows_in, group_in, (((1,), (1,)), ((), ())), precision=la...]
    concatenate x4 -> x0, other arithmetic: 12.6 us -> none  [the longest x1 10.7 us: on_device(): jnp.concatenate([product_in, product_out], axis=1)]
  transfers between devices with their start and end apart: 2 -> 0, of which waited for: 2 -> 0; matrix products, arithmetic and copies ran while one was open for 0% -> 0% of each run, Pallas kernels for 0% -> 0%
where the time goes in v1:
time: 117 us
  Pallas kernels  115 us (98%)
  local copies, waits for them, and re-layouts  1.62 us (1%)
    pallas_call x1, Pallas kernels, on_device(): pl.pallas_call(lambda *refs: kernel(total_tokens, *refs), out_shape=jax.S...  115 us

profile of v1, /device:TPU:1, one launch (start us, length us, event | category | flops | bytes accessed | tf_op | source)
XLA Modules:
  0.0 116.6 jit_solution(15120378281754806570)
XLA Ops:
  0.0 115.0 %influence.1 = f32[16,8,384]{2,1,0:T(8,128)} custom-call(bf16[192,512]{1,0:T(8,128)(2,1)} %refs_0_.1, bf16[192,512]{1,0:T(8,128)(2,1)} %refs_1_.1, bf16[16,512,512]{2,1,0:T(8,128)(2,1)} %bitcast.5, bf16[16,512,512]{2,1,0:T(8,128)(2,1)} %bitcast.6, bf16[2,4,2,256,512]{4,3,2,1,0:T(8,128)(2,1)} %bitcast.7, bf16[2,4,2,256,512]{4,3,2,1,0:T(8,128)(2,1)} %bitcast.8), custom_call_target="tpu_custom_call" | custom-call | tf_op jit(solution)/shard_map/influence/pallas_call | solution.py:325
  115.0 1.6 %copy.8 = f32[128,384]{1,0:T(8,128)} copy(f32[128,384]{1,0:T(8,128)} %bitcast.9) | data formatting | bytes 393216

commit v2 on v1

--- a/solution.py
+++ b/solution.py
@@ -30,7 +30,7 @@
     rows = X.shape[2]
     upper, lower = pl.ds(0, half), pl.ds(half, half)
 
-    keys, pending = {}, []
+    keys, pending, sent, got = {}, [], {}, set()
 
     def number(key):
         return keys.setdefault(key, len(keys))
@@ -42,14 +42,17 @@
         )
         copy.start()
         pending.append(copy)
+        sent[key] = dst
 
     def arrive(key, region, dev=None):
+        got.add(key)
         i = number(key)
         pltpu.make_async_remote_copy(
             src_ref=region, dst_ref=region, send_sem=ss.at[i], recv_sem=rs.at[i],
             device_id=dev_c if dev is None else dev, device_id_type=MESH,
         ).wait_recv()
 
+    waited = set()
     me = at(x, z, c)
     own_x = [pltpu.make_async_copy(acts[a], X.at[a, me], lx.at[a]) for a in range(2)]
     for cp in own_x:
@@ -60,12 +63,14 @@
         for n, (px, pz) in enumerate(order):
             pair = pl.ds((px * 4 + pz) * 2, 2)
             base_copies[a, n] = pltpu.make_async_copy(bases[a].at[pair], BAS.at[a, pair], lb.at[a, n])
-            base_copies[a, n].start()
     src_me = x * 2 + c
     own_a = [pltpu.make_async_copy(queries[a].at[x, :, c], A.at[a, src_me], la.at[a]) for a in range(2)]
-    for cp in own_a:
-        cp.start()
-
+
+    def load(a):
+        for n in range(8):
+            base_copies[a, n].start()
+
+    load(0)
     barrier = pltpu.get_barrier_semaphore()
     met = 0
     for d in range(1, 16):
@@ -85,7 +90,7 @@
     done_pairs = [0, 0]
 
     def rotate(a, n):
-        base_copies[a, n].wait()
+        waited.add(id(base_copies[a, n])); base_copies[a, n].wait()
         px, pz = order[n]
         first = (px * 4 + pz) * 2
         for col in range(0, 512, 256):
@@ -98,7 +103,7 @@
         done_pairs[a] += 1
 
     def open_x(a):
-        own_x[a].wait()
+        waited.add(id(own_x[a])); own_x[a].wait()
         send(("x", a), X.at[a, me], X.at[a, me], dev_x)
         send(("c", a), X.at[a, me], X.at[a, me], dev_c)
 
@@ -197,38 +202,37 @@
         arrive(("bcf", a), S.at[a, p, x * 2 + cq])
 
     def open_a(a):
+        own_a[a].start()
         send(("ac", a), queries[a].at[x, :, cq], A.at[a, src_me], dev_c)
 
-    def open_ax(a):
-        for k in range(2):
-            send_ax(a, k)
-
-    def send_ax(a, k):
+    def ax(a, k):
         pc = c if k == 0 else cq
         send(("ax", a, k), queries[a].at[xq, t, pc], A.at[a, src_me, t], {"width": at(xq, z, pc)})
 
-    def spread_a(a):
-        for k in range(2):
-            pc = c if k == 0 else cq
-            arrive(("ax", a, k), A.at[a, xq * 2 + pc, t])
-        both = pl.ds(xq * 2, 2)
-        send(("ayu", a), A.at[a, both, t], A.at[a, both, t], dev_tu)
-        send(("ayd", a), A.at[a, both, t], A.at[a, both, t], dev_td)
-
-    def spread_a2(a):
-        both = pl.ds(xq * 2, 2)
-        arrive(("ayu", a), A.at[a, both, td])
-        one = A.at[a, xq * 2, td]
-        send(("agu", a), one, one, dev_tu)
-        arrive(("ayd", a), A.at[a, both, tu])
-        two = A.at[a, xq * 2 + 1, tu]
-        send(("agd", a), two, two, dev_td)
+    def spread(a, k):
+        pc = c if k == 0 else cq
+        blk = A.at[a, xq * 2 + pc, t]
+        arrive(("ax", a, k), blk)
+        send(("ayu", a, k), blk, blk, dev_tu)
+        send(("ayd", a, k), blk, blk, dev_td)
+
+    def spread2(a):
+        blk = A.at[a, xq * 2 + c, td]
+        arrive(("ayu", a, 0), blk)
+        send(("agu", a), blk, blk, dev_tu)
+
+    def spread3(a):
+        blk = A.at[a, xq * 2 + cq, tu]
+        arrive(("ayd", a, 1), blk)
+        send(("agd", a), blk, blk, dev_td)
 
     def a_ready(a):
-        own_a[a].wait()
+        waited.add(id(own_a[a])); own_a[a].wait()
         arrive(("ac", a), A.at[a, x * 2 + cq])
-        arrive(("agu", a), A.at[a, xq * 2, tf])
-        arrive(("agd", a), A.at[a, xq * 2 + 1, tf])
+        arrive(("ayu", a, 1), A.at[a, xq * 2 + cq, td])
+        arrive(("ayd", a, 0), A.at[a, xq * 2 + c, tu])
+        arrive(("agu", a), A.at[a, xq * 2 + c, tf])
+        arrive(("agd", a), A.at[a, xq * 2 + cq, tf])
 
     def pair(a, h, zz):
         hq = q if h == 0 else p
@@ -238,32 +242,39 @@
             acc = part if acc is None else acc + part
         PS[a, h, zz] = acc[:rows] + acc[rows:]
 
-    def pairs(a, h):
+    def pf(a, h):
         pair(a, h, zf)
         send(("pfu", a, h), PS.at[a, h, zf, upper], RF.at[a, h, 0], dev_u)
         send(("pfd", a, h), PS.at[a, h, zf, lower], RF.at[a, h, 1], dev_d)
         pair(a, h, zu)
+        send(("pnu", a, h, 0), PS.at[a, h, zu, lower], RN.at[a, h, 0, lower], dev_u)
         pair(a, h, zd)
+        send(("pnd", a, h, 0), PS.at[a, h, zd, upper], RN.at[a, h, 1, upper], dev_d)
+        pair(a, h, z)
+
+    def pn(a, h):
         arrive(("pfu", a, h), RF.at[a, h, 0])
         PS[a, h, zu, upper] += RF[a, h, 0]
-        send(("pnu", a, h), PS.at[a, h, zu], RN.at[a, h, 0], dev_u)
+        send(("pnu", a, h, 1), PS.at[a, h, zu, upper], RN.at[a, h, 0, upper], dev_u)
         arrive(("pfd", a, h), RF.at[a, h, 1])
         PS[a, h, zd, lower] += RF[a, h, 1]
-        send(("pnd", a, h), PS.at[a, h, zd], RN.at[a, h, 1], dev_d)
-        pair(a, h, z)
+        send(("pnd", a, h, 1), PS.at[a, h, zd, lower], RN.at[a, h, 1, lower], dev_d)
 
     def whole(a, h):
-        arrive(("pnu", a, h), RN.at[a, h, 0])
-        arrive(("pnd", a, h), RN.at[a, h, 1])
+        for n, part in enumerate((lower, upper)):
+            arrive(("pnu", a, h, n), RN.at[a, h, 0, part])
+        for n, part in enumerate((upper, lower)):
+            arrive(("pnd", a, h, n), RN.at[a, h, 1, part])
         return PS[a, h, z] + RN[a, h, 0] + RN[a, h, 1]
 
     open_x(0)
     open_z(0)
     open_x(1)
-    open_ax(0)
-    open_a(0)
-    open_a(1)
+    ax(0, 0)
+    ax(0, 1)
+    ax(1, 0)
     step1(0)
+    load(1)
     step2(0, x, "", 2)
     step2(0, xq, "x", 4)
     open_z(1)
@@ -271,32 +282,42 @@
     step3(0, xq, "x", 7)
     squares(0)
     step1(1)
+    open_a(0)
+    spread(0, 0)
     step2(1, x, "", 2)
     scale(0)
-    open_ax(1)
-    spread_a(0)
+    ax(1, 1)
+    spread(0, 1)
     step2(1, xq, "x", 4)
+    spread2(0)
     step3(1, x, "", 6)
     step3(1, xq, "x", 7)
     squares(1)
+    spread3(0)
+    open_a(1)
+    spread(1, 0)
     share(0)
-    spread_a2(0)
+    scale(1)
     own_ready(0)
-    scale(1)
+    a_ready(0)
+    pf(0, 0)
+    pn(0, 0)
+    spread(1, 1)
     share_far(0)
-    a_ready(0)
-    pairs(0, 0)
     other_ready(0)
-    spread_a(1)
-    pairs(0, 1)
+    pf(0, 1)
+    spread2(1)
+    pn(0, 1)
+    spread3(1)
     share(1)
-    spread_a2(1)
     own_ready(1)
+    a_ready(1)
+    pf(1, 0)
+    pn(1, 0)
     share_far(1)
-    a_ready(1)
-    pairs(1, 0)
     other_ready(1)
-    pairs(1, 1)
+    pf(1, 1)
+    pn(1, 1)
     for h in range(2):
         hq = q if h == 0 else p
         PR[pl.ds(hq * rows, rows)] = whole(0, h) * whole(1, h)

time: 117 us -> 105 us (0.90)
  Pallas kernels: 115 us -> 104 us
    pallas_call x1, Pallas kernels: 115 us -> 104 us  [on_device(): pl.pallas_call(lambda *refs: kernel(total_tokens, *refs), out_shape=jax.S...]
where the time goes in v2:
time: 105 us
  Pallas kernels  104 us (99%)
  local copies, waits for them, and re-layouts  1.62 us (2%)
    pallas_call x1, Pallas kernels, on_device(): pl.pallas_call(lambda *refs: kernel(total_tokens, *refs), out_shape=jax.S...  104 us

profile of v2, /device:TPU:1, one launch (start us, length us, event | category | flops | bytes accessed | tf_op | source)
XLA Modules:
  0.0 105.2 jit_solution(3207098284668847211)
XLA Ops:
  0.0 103.5 %influence.1 = f32[16,8,384]{2,1,0:T(8,128)} custom-call(bf16[192,512]{1,0:T(8,128)(2,1)} %refs_0_.1, bf16[192,512]{1,0:T(8,128)(2,1)} %refs_1_.1, bf16[16,512,512]{2,1,0:T(8,128)(2,1)} %bitcast.5, bf16[16,512,512]{2,1,0:T(8,128)(2,1)} %bitcast.6, bf16[2,4,2,256,512]{4,3,2,1,0:T(8,128)(2,1)} %bitcast.7, bf16[2,4,2,256,512]{4,3,2,1,0:T(8,128)(2,1)} %bitcast.8), custom_call_target="tpu_custom_call" | custom-call | tf_op jit(solution)/shard_map/influence/pallas_call | solution.py:346
  103.5 1.6 %copy.8 = f32[128,384]{1,0:T(8,128)} copy(f32[128,384]{1,0:T(8,128)} %bitcast.9) | data formatting | bytes 393216

commit v3 on v2

--- a/solution.py
+++ b/solution.py
@@ -8,6 +8,7 @@
 damping = 0.1
 MESH = pl.DeviceIdType.MESH
 N_SEM = 160
+SPLIT = (False, True)
 NT = (((1,), (1,)), ((), ()))
 
 
@@ -118,18 +119,21 @@
         blk = X.at[a, at(px, pz, c)]
         send(key, blk, blk, dev_c)
 
-    def step1(a):
+    def s1(a):
         blk = X.at[a, at(xq, z, c)]
         arrive(("x", a), blk)
         send(("xzu", a), blk, blk, dev_u)
         send(("xzd", a), blk, blk, dev_d)
         to_core(("cx", a), a, xq, z)
+
+    def r1(a):
         from_core(("c", a), a, x, z)
         rotate(a, 0)
         from_core(("cx", a), a, xq, z)
         rotate(a, 1)
 
-    def step2(a, px, tag, n):
+    def s2(a, tag):
+        px = xq if tag else x
         up, down = at(px, zd, c), at(px, zu, c)
         arrive((tag + "zu", a), X.at[a, up])
         send((tag + "fu", a), X.at[a, up, upper], X.at[a, up, upper], dev_u)
@@ -137,16 +141,23 @@
         arrive((tag + "zd", a), X.at[a, down])
         send((tag + "fd", a), X.at[a, down, lower], X.at[a, down, lower], dev_d)
         to_core((tag + "czd", a), a, px, zu)
+
+    def r2(a, tag):
+        px, n = (xq, 4) if tag else (x, 2)
         from_core((tag + "czu", a), a, px, zd)
         rotate(a, n)
         from_core((tag + "czd", a), a, px, zu)
         rotate(a, n + 1)
 
-    def step3(a, px, tag, n):
+    def s3(a, tag):
+        px = xq if tag else x
         far = at(px, zf, c)
         arrive((tag + "fu", a), X.at[a, far, upper])
         arrive((tag + "fd", a), X.at[a, far, lower])
         to_core((tag + "cf", a), a, px, zf)
+
+    def r3(a, tag):
+        px, n = (xq, 7) if tag else (x, 6)
         from_core((tag + "cf", a), a, px, zf)
         rotate(a, n)
 
@@ -172,25 +183,32 @@
         send(("bo", a), blk, blk, dev_o)
         send(("bc", a), blk, blk, dev_c)
 
+    p = 1 - q
+
     his, los = pl.ds(0, rows), pl.ds(rows, rows)
-    p = 1 - q
-
-    def share(a):
-        bx = S.at[a, q, xq * 2 + c]
-        arrive(("bx", a), bx)
-        hi = S.at[a, q, xq * 2 + c, his]
-        send(("bh", a), hi, hi, dev_o)
-        send(("bcx", a), bx, bx, dev_c)
-        bo_ = S.at[a, p, xq * 2 + c]
-        arrive(("bo", a), bo_)
-        lo = S.at[a, p, xq * 2 + c, los]
-        send(("bl", a), lo, lo, dev_x)
-        send(("bco", a), bo_, bo_, dev_c)
-
-    def share_far(a):
-        arrive(("bh", a), S.at[a, p, x * 2 + c, his])
-        arrive(("bl", a), S.at[a, p, x * 2 + c, los])
+
+    def shx(a):
+        blk = S.at[a, q, xq * 2 + c]
+        arrive(("bx", a), blk)
+        part = blk if not SPLIT[a] else S.at[a, q, xq * 2 + c, his]
+        send(("bh", a), part, part, dev_o)
+        send(("bcx", a), blk, blk, dev_c)
+
+    def sho(a):
+        blk = S.at[a, p, xq * 2 + c]
+        arrive(("bo", a), blk)
+        if SPLIT[a]:
+            part = S.at[a, p, xq * 2 + c, los]
+            send(("bl", a), part, part, dev_x)
+        send(("bco", a), blk, blk, dev_c)
+
+    def sfar(a):
         blk = S.at[a, p, x * 2 + c]
+        if SPLIT[a]:
+            arrive(("bh", a), S.at[a, p, x * 2 + c, his])
+            arrive(("bl", a), S.at[a, p, x * 2 + c, los])
+        else:
+            arrive(("bh", a), blk)
         send(("bcf", a), blk, blk, dev_c)
 
     def own_ready(a):
@@ -268,53 +286,65 @@
         return PS[a, h, z] + RN[a, h, 0] + RN[a, h, 1]
 
     open_x(0)
+    open_a(1)
+    open_x(1)
+    load(1)
+    ax(0, 0)
+    ax(1, 1)
     open_z(0)
-    open_x(1)
-    ax(0, 0)
+    s1(0)
+    s2(0, "")
+    s2(0, "x")
+    s3(0, "")
+    spread(0, 0)
+    open_z(1)
+    r1(0)
+    r3(0, "")
+    s3(0, "x")
+    r2(0, "x")
+    r2(0, "")
+    r3(0, "x")
+    squares(0)
     ax(0, 1)
+    s1(1)
+    spread(1, 1)
+    spread2(0)
+    s2(1, "")
+    scale(0)
+    s2(1, "x")
+    open_a(0)
+    r1(1)
+    spread(0, 1)
+    r2(1, "")
     ax(1, 0)
-    step1(0)
-    load(1)
-    step2(0, x, "", 2)
-    step2(0, xq, "x", 4)
-    open_z(1)
-    step3(0, x, "", 6)
-    step3(0, xq, "x", 7)
-    squares(0)
-    step1(1)
-    open_a(0)
-    spread(0, 0)
-    step2(1, x, "", 2)
-    scale(0)
-    ax(1, 1)
-    spread(0, 1)
-    step2(1, xq, "x", 4)
-    spread2(0)
-    step3(1, x, "", 6)
-    step3(1, xq, "x", 7)
+    s3(1, "")
+    r2(1, "x")
+    r3(1, "")
+    s3(1, "x")
+    r3(1, "x")
     squares(1)
     spread3(0)
-    open_a(1)
+    sho(0)
+    shx(0)
     spread(1, 0)
-    share(0)
     scale(1)
     own_ready(0)
     a_ready(0)
     pf(0, 0)
+    spread3(1)
+    sfar(0)
     pn(0, 0)
-    spread(1, 1)
-    share_far(0)
     other_ready(0)
+    spread2(1)
     pf(0, 1)
-    spread2(1)
+    shx(1)
+    sho(1)
+    own_ready(1)
     pn(0, 1)
-    spread3(1)
-    share(1)
-    own_ready(1)
     a_ready(1)
     pf(1, 0)
+    sfar(1)
     pn(1, 0)
-    share_far(1)
     other_ready(1)
     pf(1, 1)
     pn(1, 1)

time: 105 us -> 96 us (0.914)
  Pallas kernels: 104 us -> 94.3 us
    pallas_call x1, Pallas kernels: 104 us -> 94.3 us  [on_device(): pl.pallas_call(lambda *refs: kernel(total_tokens, *refs), out_shape=jax.S...]
where the time goes in v3:
time: 96 us; the launch traced here: 95.9 us
  Pallas kernels  94.3 us (98%)
  local copies, waits for them, and re-layouts  1.62 us (2%)
    pallas_call x1, Pallas kernels, on_device(): pl.pallas_call(lambda *refs: kernel(total_tokens, *refs), out_shape=jax.S...  94.3 us

profile of v3, /device:TPU:1, one launch (start us, length us, event | category | flops | bytes accessed | tf_op | source)
XLA Modules:
  0.0 95.9 jit_solution(13950758419810660382)
XLA Ops:
  0.0 94.3 %influence.1 = f32[16,8,384]{2,1,0:T(8,128)} custom-call(bf16[192,512]{1,0:T(8,128)(2,1)} %refs_0_.1, bf16[192,512]{1,0:T(8,128)(2,1)} %refs_1_.1, bf16[16,512,512]{2,1,0:T(8,128)(2,1)} %bitcast.5, bf16[16,512,512]{2,1,0:T(8,128)(2,1)} %bitcast.6, bf16[2,4,2,256,512]{4,3,2,1,0:T(8,128)(2,1)} %bitcast.7, bf16[2,4,2,256,512]{4,3,2,1,0:T(8,128)(2,1)} %bitcast.8), custom_call_target="tpu_custom_call" | custom-call | tf_op jit(solution)/shard_map/influence/pallas_call | solution.py:376
  94.3 1.6 %copy.8 = f32[128,384]{1,0:T(8,128)} copy(f32[128,384]{1,0:T(8,128)} %bitcast.9) | data formatting | bytes 393216

commit v4 on v3

--- a/solution.py
+++ b/solution.py
@@ -31,7 +31,7 @@
     rows = X.shape[2]
     upper, lower = pl.ds(0, half), pl.ds(half, half)
 
-    keys, pending, sent, got = {}, [], {}, set()
+    keys, pending = {}, []
 
     def number(key):
         return keys.setdefault(key, len(keys))
@@ -43,17 +43,14 @@
         )
         copy.start()
         pending.append(copy)
-        sent[key] = dst
 
     def arrive(key, region, dev=None):
-        got.add(key)
         i = number(key)
         pltpu.make_async_remote_copy(
             src_ref=region, dst_ref=region, send_sem=ss.at[i], recv_sem=rs.at[i],
             device_id=dev_c if dev is None else dev, device_id_type=MESH,
         ).wait_recv()
 
-    waited = set()
     me = at(x, z, c)
     own_x = [pltpu.make_async_copy(acts[a], X.at[a, me], lx.at[a]) for a in range(2)]
     for cp in own_x:
@@ -91,7 +88,7 @@
     done_pairs = [0, 0]
 
     def rotate(a, n):
-        waited.add(id(base_copies[a, n])); base_copies[a, n].wait()
+        base_copies[a, n].wait()
         px, pz = order[n]
         first = (px * 4 + pz) * 2
         for col in range(0, 512, 256):
@@ -104,7 +101,7 @@
         done_pairs[a] += 1
 
     def open_x(a):
-        waited.add(id(own_x[a])); own_x[a].wait()
+        own_x[a].wait()
         send(("x", a), X.at[a, me], X.at[a, me], dev_x)
         send(("c", a), X.at[a, me], X.at[a, me], dev_c)
 
@@ -245,7 +242,7 @@
         send(("agd", a), blk, blk, dev_td)
 
     def a_ready(a):
-        waited.add(id(own_a[a])); own_a[a].wait()
+        own_a[a].wait()
         arrive(("ac", a), A.at[a, x * 2 + cq])
         arrive(("ayu", a, 1), A.at[a, xq * 2 + cq, td])
         arrive(("ayd", a, 0), A.at[a, xq * 2 + c, tu])
@@ -354,14 +351,21 @@
     ranks = 32
     pick = (
         lax.broadcasted_iota(jnp.int32, (8, 256), 1) // ranks == lax.broadcasted_iota(jnp.int32, (8, 256), 0)
-    ).astype(jnp.float32)
-    SC[w] = lax.dot_general(
-        pick, PR[...], NT, precision=lax.Precision.HIGHEST, preferred_element_type=jnp.float32
-    )
-    for d in range(1, 16):
-        send(("sc", d), SC.at[w], SC.at[w], {"width": lax.rem(w + d, 16)})
-    for d in range(1, 16):
-        arrive(("sc", d), SC.at[lax.rem(w + 16 - d, 16)])
+    ).astype(jnp.float32).astype(jnp.bfloat16)
+    left, total = PR[...], None
+    for _ in range(3):
+        term = left.astype(jnp.bfloat16)
+        left = left - term.astype(jnp.float32)
+        part = lax.dot_general(pick, term, NT, preferred_element_type=jnp.float32)
+        total = part if total is None else total + part
+    SC[w] = total
+    steps = [(dx, dz, dc) for dz in (2, 1, 3, 0) for dx in (1, 0) for dc in (0, 1) if dx + dz + dc]
+    for dx, dz, dc in steps:
+        peer = at(lax.rem(x + dx, 2), lax.rem(z + dz, 4), lax.rem(c + dc, 2))
+        send(("sc", dx, dz, dc), SC.at[w], SC.at[w], {"width": peer})
+    for dx, dz, dc in steps:
+        peer = at(lax.rem(x + dx, 2), lax.rem(z + 4 - dz, 4), lax.rem(c + dc, 2))
+        arrive(("sc", dx, dz, dc), SC.at[peer])
     out[...] = SC[...]
     for copy in pending:
         copy.wait_send()
@@ -375,7 +379,7 @@
     hbm = pl.BlockSpec(memory_space=pl.ANY)
     scores = pl.pallas_call(
         lambda *refs: kernel(total_tokens, *refs),
-        out_shape=jax.ShapeDtypeStruct((16, 8, 2 * rows), f32),
+        out_shape=pltpu.VMEM((16, 8, 2 * rows), f32),
         in_specs=[hbm] * 6,
         out_specs=pl.BlockSpec(memory_space=pltpu.VMEM),
         scratch_shapes=[

time: 96 us -> 94.2 us (0.981)
  no operation moved by 1% of the time
where the time goes in v4:
time: 94.2 us; the launch traced here: 94.1 us
  Pallas kernels  93.4 us (99%)
    pallas_call x1, Pallas kernels, on_device(): pl.pallas_call(lambda *refs: kernel(total_tokens, *refs), out_shape=pltpu...  93.4 us

profile of v4, /device:TPU:1, one launch (start us, length us, event | category | flops | bytes accessed | tf_op | source)
XLA Modules:
  0.0 94.1 jit_solution(9824428864389900379)
XLA Ops:
  0.0 93.4 %influence.1 = f32[16,8,384]{2,1,0:T(8,128)S(1)} custom-call(bf16[192,512]{1,0:T(8,128)(2,1)} %refs_0_.1, bf16[192,512]{1,0:T(8,128)(2,1)} %refs_1_.1, bf16[16,512,512]{2,1,0:T(8,128)(2,1)} %bitcast.6, bf16[16,512,512]{2,1,0:T(8,128)(2,1)} %bitcast.7, bf16[2,4,2,256,512]{4,3,2,1,0:T(8,128)(2,1)} %bitcast.8, bf16[2,4,2,256,512]{4,3,2,1,0:T(8,128)(2,1)} %bitcast.9), custom_call_target="tpu_custom_call" | custom-call | tf_op jit(solution)/shard_map/influence/pallas_call | solution.py:380
  93.5 0.7 copy.8

commit v5 on v4

--- a/solution.py
+++ b/solution.py
@@ -283,13 +283,12 @@
         return PS[a, h, z] + RN[a, h, 0] + RN[a, h, 1]
 
     open_x(0)
-    open_a(1)
     open_x(1)
-    load(1)
     ax(0, 0)
-    ax(1, 1)
+    ax(0, 1)
     open_z(0)
     s1(0)
+    load(1)
     s2(0, "")
     s2(0, "x")
     s3(0, "")
@@ -302,16 +301,16 @@
     r2(0, "")
     r3(0, "x")
     squares(0)
-    ax(0, 1)
+    ax(1, 1)
     s1(1)
-    spread(1, 1)
+    spread(0, 1)
     spread2(0)
     s2(1, "")
     scale(0)
     s2(1, "x")
     open_a(0)
     r1(1)
-    spread(0, 1)
+    spread(1, 1)
     r2(1, "")
     ax(1, 0)
     s3(1, "")
@@ -320,6 +319,7 @@
     s3(1, "x")
     r3(1, "x")
     squares(1)
+    open_a(1)
     spread3(0)
     sho(0)
     shx(0)

time: 94.2 us -> 94.2 us (level)
  no operation moved by 1% of the time
where the time goes in v5:
time: 94.2 us; the launch traced here: 94.1 us
  Pallas kernels  93.4 us (99%)
    pallas_call x1, Pallas kernels, on_device(): pl.pallas_call(lambda *refs: kernel(total_tokens, *refs), out_shape=pltpu...  93.4 us

profile of v5, /device:TPU:1, one launch (start us, length us, event | category | flops | bytes accessed | tf_op | source)
XLA Modules:
  0.0 94.1 jit_solution(11926937040136520375)
XLA Ops:
  0.0 93.4 %influence.1 = f32[16,8,384]{2,1,0:T(8,128)S(1)} custom-call(bf16[192,512]{1,0:T(8,128)(2,1)} %refs_0_.1, bf16[192,512]{1,0:T(8,128)(2,1)} %refs_1_.1, bf16[16,512,512]{2,1,0:T(8,128)(2,1)} %bitcast.6, bf16[16,512,512]{2,1,0:T(8,128)(2,1)} %bitcast.7, bf16[2,4,2,256,512]{4,3,2,1,0:T(8,128)(2,1)} %bitcast.8, bf16[2,4,2,256,512]{4,3,2,1,0:T(8,128)(2,1)} %bitcast.9), custom_call_target="tpu_custom_call" | custom-call | tf_op jit(solution)/shard_map/influence/pallas_call | solution.py:380
  93.5 0.7 copy.8
